TPU v7x, 512 devices: a whole 4x4x16 slice. The times are simulated.
512 devices in a mesh: dir: 8 (over x, core), texel: 64 (over z, y).
Axes of the slice: x: 4, y: 4, z: 16, core: 2. Of those that a mesh axis runs over, the one named last changes fastest.
Arguments:
- texels: bfloat16 [4096, 50176], P('texel', 'dir'), may hold values from -6 to 6
- labels: int32 [4096, 1], P('texel'), may hold values from 0 to 127; in each aligned block of 64 rows (0 to 63, 64 to 127, ...) at most 2 rows name the same one
- start_basis: bfloat16 [64, 50176], P(None, 'dir'), may hold values from -0.02734375 to 0.02734375
Outputs:
- coefficients: float32 [4096, 64], P('texel')
- bases: bfloat16 [128, 64, 50176], P('texel', None, 'dir')
Inputs may be any that keep to these rules, and one draw needn't show every extreme that they name: `labels`: among the rows of one index of texel (an aligned block of 64 rows) no cluster is named by more than 2 rows, a bound that some block reaches in every draw.
All inputs are finite; a program needn't handle non-finite values.
Results may differ from a plain program's by a relative error of at most 0.012.
Values may be sent and summed in bfloat16 or wider, within the bound.
A program may use at most 64 MiB of HBM per device.

v0:
```python
import jax
import jax.numpy as jnp
from jax import lax
from jax.sharding import PartitionSpec as P

COLS = 50176
K = 64
CL_DEV = 2
ITERS = 2
ridge_share = 0.05


def per_device(texels, labels, start_basis):
    row_count = texels.shape[0]
    col_width = texels.shape[1]
    groups = lax.axis_size("texel")
    slot_cap = max(2, 2 * row_count // (CL_DEV * groups))
    label_col = labels[:, 0]
    owners = label_col // CL_DEV
    local_idx = label_col % CL_DEV
    row_ids = jnp.arange(row_count, dtype=jnp.int32)
    matches = (label_col[None, :] == label_col[:, None]) & (row_ids[None, :] < row_ids[:, None])
    slot_rank = jnp.sum(matches.astype(jnp.int32), axis=1)
    slot_of_row = local_idx * (groups * slot_cap) + owners * slot_cap + slot_rank
    total_slots = CL_DEV * groups * slot_cap
    slot_ids = jnp.arange(total_slots, dtype=jnp.int32)
    slot_hit = slot_of_row[None, :] == slot_ids[:, None]
    source_row = jnp.sum(jnp.where(slot_hit, row_ids[None, :], 0), axis=1)
    filled = jnp.any(slot_hit, axis=1)
    outgoing = jnp.where(
        filled[:, None], jnp.take(texels, source_row, axis=0), jnp.zeros((), texels.dtype)
    )
    outgoing = outgoing.reshape(CL_DEV, groups * slot_cap, col_width)
    received = lax.all_to_all(outgoing, "texel", split_axis=1, concat_axis=1, tiled=True)
    ridge_term = jnp.float32(ridge_share * COLS)
    identity = jnp.broadcast_to(jnp.eye(K, dtype=jnp.float32), (CL_DEV, K, K))
    basis_now = jnp.broadcast_to(start_basis, (CL_DEV, K, col_width))
    highest = lax.Precision.HIGHEST
    for sweep in range(ITERS):
        local_proj = jnp.einsum(
            "crw,ckw->crk", received, basis_now, preferred_element_type=jnp.float32
        )
        summed_proj = lax.psum(local_proj, "dir")
        projected = summed_proj.astype(jnp.bfloat16)
        widened = jnp.einsum(
            "crk,crw->ckw", projected, received, preferred_element_type=jnp.float32
        ) + ridge_term * basis_now.astype(jnp.float32)
        gram_mat = lax.psum(
            jnp.einsum(
                "ckw,clw->ckl",
                widened,
                widened,
                precision=highest,
                preferred_element_type=jnp.float32,
            ),
            "dir",
        )
        lower_tri = jnp.linalg.cholesky(gram_mat)
        inverse = jax.scipy.linalg.solve_triangular(lower_tri, identity, lower=True)
        basis_now = jnp.einsum(
            "ckl,clw->ckw", inverse, widened, precision=highest, preferred_element_type=jnp.float32
        ).astype(jnp.bfloat16)
    partial_value = jnp.einsum(
        "crw,ckw->crk", received, basis_now, preferred_element_type=jnp.float32
    )
    summed = lax.psum(partial_value.astype(jnp.bfloat16), "dir").astype(jnp.float32)
    returned = lax.all_to_all(
        summed.astype(jnp.bfloat16), "texel", split_axis=1, concat_axis=1, tiled=True
    ).astype(summed.dtype)
    coefficients = returned.reshape(total_slots, K)[slot_of_row]
    return (coefficients, basis_now)


def solution(mesh):
    in_specs = (P("texel", "dir"), P("texel", None), P(None, "dir"))
    out_specs = (P("texel", None), P("texel", None, "dir"))
    return jax.shard_map(
        per_device, mesh=mesh, in_specs=in_specs, out_specs=out_specs, check_vma=False
    )
```

profile of v0, /device:TPU:8, one launch (start us, length us, event | category | flops | bytes accessed | tf_op | source)
XLA Modules:
  0.0 404.1 jit_solution(9749141329993377410)
XLA Ops:
  2.8 4.2 %gather_fusion = bf16[256,6272]{1,0:T(8,128)(2,1)} fusion(bf16[64,6272]{1,0:T(8,128)(2,1)S(1)} %copy-done, s32[1024]{0:T(1024)S(1)} %pad_clamp_fusion.1), kind=kCustom, calls=%fused_computation | custom fusion | bytes 6423552 | tf_op jit(solution)/shard_map/jit(_take)/gather | solution.py:31
  7.0 8.2 %broadcast_select_fusion.1 = bf16[2,128,6272]{2,0,1:T(2,128)(2,1)} fusion(pred[2,128]{0,1:T(8,128)(4,1)S(1)} %copy.64, pred[2,128]{0,1:T(8,128)(4,1)S(1)} %copy.65, bf16[2,128,6272]{2,1,0:T(8,128)(2,1)} %bitcast.47), kind=kLoop, calls=%fused_computation.7 | loop fusion | flops 3211264 | bytes 6423040 | tf_op jit(solution)/shard_map/jit(_where)/select_n | solution.py:30
  15.2 19.0 %all-to-all-start = ((bf16[2,128,6272]{2,0,1:T(2,128)(2,1)}), bf16[2,128,6272]{2,0,1:T(2,128)(2,1)}, u32[]{:S(2)}, u32[]{:S(2)}) async-start(bf16[2,128,6272]{2,0,1:T(2,128)(2,1)} %broadcast_select_fusion.1), calls=%async_computation | async-start | bytes 6422528 | tf_op jit(solution)/shard_map/all_to_all | solution.py:34
  34.4 147.6 %all-to-all-done = bf16[2,128,6272]{2,0,1:T(2,128)(2,1)} async-done(((bf16[2,128,6272]{2,0,1:T(2,128)(2,1)}), bf16[2,128,6272]{2,0,1:T(2,128)(2,1)}, u32[]{:S(2)}, u32[]{:S(2)}) %all-to-all-start) | async-done | bytes 3211296 | tf_op jit(solution)/shard_map/all_to_all | solution.py:34
  182.0 3.1 fusion.2
  185.1 24.1 %psum.35 = bf16[2,128,64]{1,2,0:T(8,128)(2,1)S(1)} all-reduce(f32[2,128,64]{1,2,0:T(8,128)S(1)} %fusion.2), channel_id=1, replica_groups=mesh['dir'=8,'texel'=64] {'dir'}, use_global_device_ids=true, to_apply=%region_3.4 | all-reduce | flops 16384 | bytes 98304 | tf_op jit(solution)/shard_map/psum | solution.py:43
  209.3 2.7 convolution_add_fusion.1
  213.7 3.1 fusion.32
  216.8 23.9 %psum.36 = f32[2,64,64]{1,2,0:T(8,128)S(1)} all-reduce(f32[2,64,64]{1,2,0:T(8,128)S(1)} %fusion.32), channel_id=1, replica_groups=mesh['dir'=8,'texel'=64] {'dir'}, use_global_device_ids=true, to_apply=%region_4.5 | all-reduce | flops 8192 | bytes 65536 | tf_op jit(solution)/shard_map/psum | solution.py:48
  240.9 11.7 %custom-call.8 = f32[2,64,64]{2,1,0:T(8,128)S(1)} custom-call(f32[2,64,64]{2,1,0:T(8,128)S(1)} %fusion.17), custom_call_target="Cholesky" | custom-call | tf_op jit(solution)/shard_map/jit(cholesky)/cholesky | solution.py:58
  252.9 9.8 %custom-call.9 = f32[2,1,64,64]{2,3,1,0:T(8,128)S(1)} custom-call(f32[2,1,64,64]{3,2,1,0:T(8,128)S(1)} %select_bitcast_fusion.1), custom_call_target="InvertDiagBlocksLowerTriangular" | custom-call | tf_op jit(solution)/shard_map/jit(_solve_triangular)/vmap()/triangular_solve | solution.py:59
  263.0 4.7 %convolution_convert_fusion.1 = bf16[2,64,6272]{2,1,0:T(8,128)(2,1)S(1)} fusion(f32[2,64,64]{2,1,0:T(8,128)S(1)} %fusion.15, f32[2,64,6272]{2,1,0:T(8,128)} %copy-done.2), kind=kOutput, calls=%fused_computation.5 | convolution fusion | flops 617365504 | bytes 4849664 | tf_op jit(solution)/shard_map/ckl,clw->ckw/dot_general | solution.py:60
  267.7 3.1 fusion.4
  270.9 24.2 %psum.37 = bf16[2,128,64]{1,2,0:T(8,128)(2,1)S(1)} all-reduce(f32[2,128,64]{1,2,0:T(8,128)S(1)} %fusion.4), channel_id=1, replica_groups=mesh['dir'=8,'texel'=64] {'dir'}, use_global_device_ids=true, to_apply=%region_7.10 | all-reduce | flops 16384 | bytes 98304 | tf_op jit(solution)/shard_map/psum | solution.py:43
  295.1 2.6 convolution_add_fusion
  299.4 3.1 fusion.33
  302.5 23.9 %psum.38 = f32[2,64,64]{1,2,0:T(8,128)S(1)} all-reduce(f32[2,64,64]{1,2,0:T(8,128)S(1)} %fusion.33), channel_id=1, replica_groups=mesh['dir'=8,'texel'=64] {'dir'}, use_global_device_ids=true, to_apply=%region_8.11 | all-reduce | flops 8192 | bytes 65536 | tf_op jit(solution)/shard_map/psum | solution.py:48
  326.6 11.7 %custom-call.10 = f32[2,64,64]{2,1,0:T(8,128)S(1)} custom-call(f32[2,64,64]{2,1,0:T(8,128)S(1)} %fusion.14), custom_call_target="Cholesky" | custom-call | tf_op jit(solution)/shard_map/jit(cholesky)/cholesky | solution.py:58
  338.6 9.8 %custom-call.11 = f32[2,1,64,64]{2,3,1,0:T(8,128)S(1)} custom-call(f32[2,1,64,64]{3,2,1,0:T(8,128)S(1)} %select_bitcast_fusion), custom_call_target="InvertDiagBlocksLowerTriangular" | custom-call | tf_op jit(solution)/shard_map/jit(_solve_triangular)/vmap()/triangular_solve | solution.py:59
  348.7 4.7 %convolution_convert_fusion = bf16[2,64,6272]{2,1,0:T(8,128)(2,1)S(1)} fusion(f32[2,64,64]{2,1,0:T(8,128)S(1)} %fusion.12, f32[2,64,6272]{2,1,0:T(8,128)} %copy-done.1), kind=kOutput, calls=%fused_computation.4 | convolution fusion | flops 617365504 | bytes 4849664 | tf_op jit(solution)/shard_map/ckl,clw->ckw/dot_general | solution.py:60
  353.5 3.7 fusion.8
  357.2 23.6 %psum.39 = bf16[2,128,64]{1,2,0:T(8,128)(2,1)S(1)} all-reduce(bf16[2,128,64]{1,2,0:T(8,128)(2,1)S(1)} %fusion.8), channel_id=1, replica_groups=mesh['dir'=8,'texel'=64] {'dir'}, use_global_device_ids=true, to_apply=%region_9.12 | all-reduce | flops 16384 | bytes 65536 | tf_op jit(solution)/shard_map/psum | solution.py:66
  381.7 7.3 %all-to-all-start.1 = ((bf16[64,2,128]{2,1,0:T(2,128)(2,1)}), bf16[64,2,128]{2,1,0:T(2,128)(2,1)S(1)}, u32[]{:S(2)}, u32[]{:S(2)}) async-start(bf16[64,2,128]{2,1,0:T(2,128)(2,1)} %reshape.126), calls=%async_computation.1 | async-start | bytes 65536 | tf_op jit(solution)/shard_map/all_to_all | solution.py:67
  389.0 13.6 %all-to-all-done.1 = bf16[64,2,128]{2,1,0:T(2,128)(2,1)S(1)} async-done(((bf16[64,2,128]{2,1,0:T(2,128)(2,1)}), bf16[64,2,128]{2,1,0:T(2,128)(2,1)S(1)}, u32[]{:S(2)}, u32[]{:S(2)}) %all-to-all-start.1) | async-done | bytes 32800 | tf_op jit(solution)/shard_map/all_to_all | solution.py:67
  (45 shorter events, 9.2 us)
Async XLA Ops:
  0.6 2.1 copy-start
  15.2 19.1 %copy-start.4 = (bf16[64,6272]{1,0:T(8,128)(2,1)S(1)}, bf16[64,6272]{1,0:T(8,128)(2,1)}, u32[]{:S(2)}) copy-start(bf16[64,6272]{1,0:T(8,128)(2,1)} %param.8) | copy-start | bytes 2408452
  15.2 166.8 %all-to-all-start = ((bf16[2,128,6272]{2,0,1:T(2,128)(2,1)}), bf16[2,128,6272]{2,0,1:T(2,128)(2,1)}, u32[]{:S(2)}, u32[]{:S(2)}) async-start(bf16[2,128,6272]{2,0,1:T(2,128)(2,1)} %broadcast_select_fusion.1), calls=%async_computation | async-start | bytes 6422528 | tf_op jit(solution)/shard_map/all_to_all | solution.py:34
  212.0 1.7 copy-start.2
  297.7 1.7 copy-start.1
  353.4 50.7 %copy-start.3 = (bf16[2,64,6272]{2,1,0:T(8,128)(2,1)}, bf16[2,64,6272]{2,1,0:T(8,128)(2,1)S(1)}, u32[]{:S(2)}) copy-start(bf16[2,64,6272]{2,1,0:T(8,128)(2,1)S(1)} %convolution_convert_fusion) | copy-start | bytes 4816900
  353.5 35.5 %copy-start.5 = (s32[64,1]{0,1:T(1,128)S(1)}, s32[64,1]{0,1:T(1,128)}, u32[]{:S(2)}) copy-start(s32[64,1]{0,1:T(1,128)} %param.7) | copy-start | bytes 772
  381.7 21.0 %all-to-all-start.1 = ((bf16[64,2,128]{2,1,0:T(2,128)(2,1)}), bf16[64,2,128]{2,1,0:T(2,128)(2,1)S(1)}, u32[]{:S(2)}, u32[]{:S(2)}) async-start(bf16[64,2,128]{2,1,0:T(2,128)(2,1)} %reshape.126), calls=%async_computation.1 | async-start | bytes 65536 | tf_op jit(solution)/shard_map/all_to_all | solution.py:67
where the time goes:
time: 405 us; the launch traced here: 404 us
  waiting for transfers between devices  161 us (40%)
  blocking collectives  120 us (30%)
  other arithmetic  53.8 us (13%)
  matrix products  31.7 us (8%)
  starting transfers between devices  26.3 us (6%)
  local copies, waits for them, and re-layouts  10.4 us (3%)
    all_to_all x1, waiting for transfers between devices, per_device(): lax.all_to_all(outgoing, 'texel', split_axis=1, concat_axis=1, tiled=True)  148 us
    psum x2, blocking collectives, per_device(): summed_proj = lax.psum(local_proj, 'dir')  48.3 us
    psum x2, blocking collectives, per_device(): lax.psum(jnp.einsum('ckw,clw->ckl', widened, widened, precision=highest,...  47.9 us
    another operation x7, other arithmetic, per_device(): lower_tri = jnp.linalg.cholesky(gram_mat)  23.8 us
    psum x1, blocking collectives, per_device(): lax.psum(partial_value.astype(jnp.bfloat16), 'dir').astype(jnp.float32)  23.6 us
    another operation x5, other arithmetic, per_device(): inverse = jax.scipy.linalg.solve_triangular(lower_tri, identity, lower=True)  19.8 us
    all_to_all x1, starting transfers between devices, per_device(): lax.all_to_all(outgoing, 'texel', split_axis=1, concat_axis=1, tiled=True)  19 us
    all_to_all x1, waiting for transfers between devices, per_device(): lax.all_to_all(summed.astype(jnp.bfloat16), 'texel', split_axis=1, concat...  13.6 us
  transfers between devices with their start and end apart: 2, of which 2 were waited for; matrix products, arithmetic and copies ran while one was open for 0% of the time, Pallas kernels for 0%

commit v1 on v0

--- a/solution.py
+++ b/solution.py
@@ -40,7 +40,8 @@
         local_proj = jnp.einsum(
             "crw,ckw->crk", received, basis_now, preferred_element_type=jnp.float32
         )
-        summed_proj = lax.psum(local_proj, "dir")
+        blocks = lax.all_gather(local_proj, "dir")
+        summed_proj = jnp.sum(blocks, axis=0)
         projected = summed_proj.astype(jnp.bfloat16)
         widened = jnp.einsum(
             "crk,crw->ckw", projected, received, preferred_element_type=jnp.float32

time: 405 us -> 385 us (0.951)
  blocking collectives: 120 us -> 101 us
    psum x2 -> x0, blocking collectives: 48.3 us -> none  [per_device(): summed_proj = lax.psum(local_proj, 'dir')]
    all_gather x0 -> x2, blocking collectives: none -> 27 us  [per_device(): blocks = lax.all_gather(local_proj, 'dir')]
where the time goes in v1:
time: 385 us; the launch traced here: 384 us
  waiting for transfers between devices  161 us (42%)
  blocking collectives  101 us (26%)
  other arithmetic  53.8 us (14%)
  matrix products  31.7 us (8%)
  starting transfers between devices  25 us (6%)
  local copies, waits for them, and re-layouts  10.4 us (3%)
    all_to_all x1, waiting for transfers between devices, per_device(): lax.all_to_all(outgoing, 'texel', split_axis=1, concat_axis=1, tiled=True)  148 us
    psum x2, blocking collectives, per_device(): lax.psum(jnp.einsum('ckw,clw->ckl', widened, widened, precision=highest,...  50.4 us
    all_gather x2, blocking collectives, per_device(): blocks = lax.all_gather(local_proj, 'dir')  27 us
    another operation x7, other arithmetic, per_device(): lower_tri = jnp.linalg.cholesky(gram_mat)  23.8 us
    psum x1, blocking collectives, per_device(): lax.psum(partial_value.astype(jnp.bfloat16), 'dir').astype(jnp.float32)  23.6 us
    another operation x5, other arithmetic, per_device(): inverse = jax.scipy.linalg.solve_triangular(lower_tri, identity, lower=True)  19.8 us
    all_to_all x1, starting transfers between devices, per_device(): lax.all_to_all(outgoing, 'texel', split_axis=1, concat_axis=1, tiled=True)  19 us
    all_to_all x1, waiting for transfers between devices, per_device(): lax.all_to_all(summed.astype(jnp.bfloat16), 'texel', split_axis=1, concat...  13.6 us
  transfers between devices with their start and end apart: 2, of which 2 were waited for; matrix products, arithmetic and copies ran while one was open for 0% of the time, Pallas kernels for 0%

profile of v1, /device:TPU:8, one launch (start us, length us, event | category | flops | bytes accessed | tf_op | source)
XLA Modules:
  0.0 384.1 jit_solution(2799998553661570240)
XLA Ops:
  2.8 4.2 %gather_fusion = bf16[256,6272]{1,0:T(8,128)(2,1)} fusion(bf16[64,6272]{1,0:T(8,128)(2,1)S(1)} %copy-done, s32[1024]{0:T(1024)S(1)} %pad_clamp_fusion.1), kind=kCustom, calls=%fused_computation | custom fusion | bytes 6423552 | tf_op jit(solution)/shard_map/jit(_take)/gather | solution.py:31
  7.0 8.2 %broadcast_select_fusion.1 = bf16[2,128,6272]{2,0,1:T(2,128)(2,1)} fusion(pred[2,128]{0,1:T(8,128)(4,1)S(1)} %copy.64, pred[2,128]{0,1:T(8,128)(4,1)S(1)} %copy.65, bf16[2,128,6272]{2,1,0:T(8,128)(2,1)} %bitcast.49), kind=kLoop, calls=%fused_computation.7 | loop fusion | flops 3211264 | bytes 6423040 | tf_op jit(solution)/shard_map/jit(_where)/select_n | solution.py:30
  15.2 19.0 %all-to-all-start = ((bf16[2,128,6272]{2,0,1:T(2,128)(2,1)}), bf16[2,128,6272]{2,0,1:T(2,128)(2,1)}, u32[]{:S(2)}, u32[]{:S(2)}) async-start(bf16[2,128,6272]{2,0,1:T(2,128)(2,1)} %broadcast_select_fusion.1), calls=%async_computation | async-start | bytes 6422528 | tf_op jit(solution)/shard_map/all_to_all | solution.py:34
  34.4 147.6 %all-to-all-done = bf16[2,128,6272]{2,0,1:T(2,128)(2,1)} async-done(((bf16[2,128,6272]{2,0,1:T(2,128)(2,1)}), bf16[2,128,6272]{2,0,1:T(2,128)(2,1)}, u32[]{:S(2)}, u32[]{:S(2)}) %all-to-all-start) | async-done | bytes 3211296 | tf_op jit(solution)/shard_map/all_to_all | solution.py:34
  182.0 3.1 fusion.2
  185.1 13.6 %all-gather = f32[16,128,64]{1,2,0:T(8,128)S(1)} all-gather(f32[2,128,64]{1,2,0:T(8,128)S(1)} %fusion.2), channel_id=2, replica_groups=mesh['dir'=8,'texel'=64] {'dir'}, dimensions={0}, use_global_device_ids=true | all-gather | bytes 589824 | tf_op jit(solution)/shard_map/all_gather | solution.py:43
  198.8 2.7 convolution_add_fusion.1
  203.2 3.1 fusion.32
  206.4 26.2 %psum.21 = f32[2,64,64]{1,2,0:T(8,128)S(1)} all-reduce(f32[2,64,64]{1,2,0:T(8,128)S(1)} %fusion.32), channel_id=1, replica_groups=mesh['dir'=8,'texel'=64] {'dir'}, use_global_device_ids=true, to_apply=%region_4.5 | all-reduce | flops 8192 | bytes 65536 | tf_op jit(solution)/shard_map/psum | solution.py:49
  232.7 11.7 %custom-call.8 = f32[2,64,64]{2,1,0:T(8,128)S(1)} custom-call(f32[2,64,64]{2,1,0:T(8,128)S(1)} %fusion.17), custom_call_target="Cholesky" | custom-call | tf_op jit(solution)/shard_map/jit(cholesky)/cholesky | solution.py:59
  244.7 9.8 %custom-call.9 = f32[2,1,64,64]{2,3,1,0:T(8,128)S(1)} custom-call(f32[2,1,64,64]{3,2,1,0:T(8,128)S(1)} %select_bitcast_fusion.1), custom_call_target="InvertDiagBlocksLowerTriangular" | custom-call | tf_op jit(solution)/shard_map/jit(_solve_triangular)/vmap()/triangular_solve | solution.py:60
  254.8 4.7 %convolution_convert_fusion.1 = bf16[2,64,6272]{2,1,0:T(8,128)(2,1)S(1)} fusion(f32[2,64,64]{2,1,0:T(8,128)S(1)} %fusion.15, f32[2,64,6272]{2,1,0:T(8,128)} %copy-done.2), kind=kOutput, calls=%fused_computation.5 | convolution fusion | flops 617365504 | bytes 4849664 | tf_op jit(solution)/shard_map/ckl,clw->ckw/dot_general | solution.py:61
  259.6 3.1 fusion.4
  262.7 13.3 %all-gather.1 = f32[16,128,64]{1,2,0:T(8,128)S(1)} all-gather(f32[2,128,64]{1,2,0:T(8,128)S(1)} %fusion.4), channel_id=3, replica_groups=mesh['dir'=8,'texel'=64] {'dir'}, dimensions={0}, use_global_device_ids=true | all-gather | bytes 589824 | tf_op jit(solution)/shard_map/all_gather | solution.py:43
  276.1 2.6 convolution_add_fusion
  280.4 3.1 fusion.33
  283.6 24.2 %psum.22 = f32[2,64,64]{1,2,0:T(8,128)S(1)} all-reduce(f32[2,64,64]{1,2,0:T(8,128)S(1)} %fusion.33), channel_id=1, replica_groups=mesh['dir'=8,'texel'=64] {'dir'}, use_global_device_ids=true, to_apply=%region_8.11 | all-reduce | flops 8192 | bytes 65536 | tf_op jit(solution)/shard_map/psum | solution.py:49
  307.9 11.7 %custom-call.10 = f32[2,64,64]{2,1,0:T(8,128)S(1)} custom-call(f32[2,64,64]{2,1,0:T(8,128)S(1)} %fusion.14), custom_call_target="Cholesky" | custom-call | tf_op jit(solution)/shard_map/jit(cholesky)/cholesky | solution.py:59
  319.8 9.8 %custom-call.11 = f32[2,1,64,64]{2,3,1,0:T(8,128)S(1)} custom-call(f32[2,1,64,64]{3,2,1,0:T(8,128)S(1)} %select_bitcast_fusion), custom_call_target="InvertDiagBlocksLowerTriangular" | custom-call | tf_op jit(solution)/shard_map/jit(_solve_triangular)/vmap()/triangular_solve | solution.py:60
  330.0 4.7 %convolution_convert_fusion = bf16[2,64,6272]{2,1,0:T(8,128)(2,1)S(1)} fusion(f32[2,64,64]{2,1,0:T(8,128)S(1)} %fusion.12, f32[2,64,6272]{2,1,0:T(8,128)} %copy-done.1), kind=kOutput, calls=%fused_computation.4 | convolution fusion | flops 617365504 | bytes 4849664 | tf_op jit(solution)/shard_map/ckl,clw->ckw/dot_general | solution.py:61
  334.8 3.7 fusion.8
  338.5 23.6 %psum.23 = bf16[2,128,64]{1,2,0:T(8,128)(2,1)S(1)} all-reduce(bf16[2,128,64]{1,2,0:T(8,128)(2,1)S(1)} %fusion.8), channel_id=1, replica_groups=mesh['dir'=8,'texel'=64] {'dir'}, use_global_device_ids=true, to_apply=%region_9.12 | all-reduce | flops 16384 | bytes 65536 | tf_op jit(solution)/shard_map/psum | solution.py:67
  363.0 6.0 %all-to-all-start.1 = ((bf16[64,2,128]{2,1,0:T(2,128)(2,1)}), bf16[64,2,128]{2,1,0:T(2,128)(2,1)S(1)}, u32[]{:S(2)}, u32[]{:S(2)}) async-start(bf16[64,2,128]{2,1,0:T(2,128)(2,1)} %reshape.128), calls=%async_computation.1 | async-start | bytes 65536 | tf_op jit(solution)/shard_map/all_to_all | solution.py:68
  369.0 13.6 %all-to-all-done.1 = bf16[64,2,128]{2,1,0:T(2,128)(2,1)S(1)} async-done(((bf16[64,2,128]{2,1,0:T(2,128)(2,1)}), bf16[64,2,128]{2,1,0:T(2,128)(2,1)S(1)}, u32[]{:S(2)}, u32[]{:S(2)}) %all-to-all-start.1) | async-done | bytes 32800 | tf_op jit(solution)/shard_map/all_to_all | solution.py:68
  (47 shorter events, 9.3 us)
Async XLA Ops:
  0.6 2.1 copy-start
  15.2 19.1 %copy-start.4 = (bf16[64,6272]{1,0:T(8,128)(2,1)S(1)}, bf16[64,6272]{1,0:T(8,128)(2,1)}, u32[]{:S(2)}) copy-start(bf16[64,6272]{1,0:T(8,128)(2,1)} %param.8) | copy-start | bytes 2408452
  15.2 166.8 %all-to-all-start = ((bf16[2,128,6272]{2,0,1:T(2,128)(2,1)}), bf16[2,128,6272]{2,0,1:T(2,128)(2,1)}, u32[]{:S(2)}, u32[]{:S(2)}) async-start(bf16[2,128,6272]{2,0,1:T(2,128)(2,1)} %broadcast_select_fusion.1), calls=%async_computation | async-start | bytes 6422528 | tf_op jit(solution)/shard_map/all_to_all | solution.py:34
  201.5 1.7 copy-start.2
  278.7 1.7 copy-start.1
  334.7 49.3 %copy-start.3 = (bf16[2,64,6272]{2,1,0:T(8,128)(2,1)}, bf16[2,64,6272]{2,1,0:T(8,128)(2,1)S(1)}, u32[]{:S(2)}) copy-start(bf16[2,64,6272]{2,1,0:T(8,128)(2,1)S(1)} %convolution_convert_fusion) | copy-start | bytes 4816900
  334.7 34.2 %copy-start.5 = (s32[64,1]{0,1:T(1,128)S(1)}, s32[64,1]{0,1:T(1,128)}, u32[]{:S(2)}) copy-start(s32[64,1]{0,1:T(1,128)} %param.7) | copy-start | bytes 772
  363.0 19.6 %all-to-all-start.1 = ((bf16[64,2,128]{2,1,0:T(2,128)(2,1)}), bf16[64,2,128]{2,1,0:T(2,128)(2,1)S(1)}, u32[]{:S(2)}, u32[]{:S(2)}) async-start(bf16[64,2,128]{2,1,0:T(2,128)(2,1)} %reshape.128), calls=%async_computation.1 | async-start | bytes 65536 | tf_op jit(solution)/shard_map/all_to_all | solution.py:68
